TPU v7x, 256 devices: a whole 4x4x8 slice. The times are simulated.
256 devices in a mesh: dp: 2 (over core), ctx: 32 (over z, x), mp: 4 (over y).
Axes of the slice: x: 4, y: 4, z: 8, core: 2. Of those that a mesh axis runs over, the one named last changes fastest.
Arguments:
- image_states: bfloat16 [2, 8192, 8192], P('dp', 'ctx', 'mp'), may hold values from -6 to 6
- place_index: int32 [2, 8192], P('dp'), may hold values from 0 to 16383, as said below
- doc_ids: int32 [2, 16384], P('dp'), may hold values from 0 to 127, never falling along the last dimension, each value on 1 to 512 neighbouring positions
- queries: bfloat16 [2, 16384, 4096], P('dp', 'ctx', 'mp'), may hold values from -160 to 160
- text_kv: bfloat16 [2, 16384, 1024], P('dp', 'ctx', 'mp'), may hold values from -5.5 to 5.5
- kv_weight: bfloat16 [4, 8192, 256], P('mp'), may hold values from -0.0625 to 0.0625
- d_out: bfloat16 [2, 16384, 4096], P('dp', 'ctx', 'mp'), may hold values from -6 to 6
Outputs:
- attn_out: bfloat16 [2, 16384, 4096], P('dp', 'ctx', 'mp')
- image_grad: bfloat16 [2, 8192, 8192], P('dp', 'ctx', 'mp')
- kv_weight_grad: float32 [4, 8192, 256], P('mp', 'ctx')
Inputs may be any that keep to these rules, and one draw needn't show every extreme that they name: `place_index`: images are whole blocks of 16 image tokens, consecutive in a vision rank's order and placed on 16 consecutive positions aligned to 16; every context shard of 512 positions holds exactly 256 image tokens; no position gets two image tokens; at most 16 image tokens of one vision rank lie in one context shard, and in every draw some vision rank places exactly 16 in some shard.
All inputs are finite; a program needn't handle non-finite values.
Results may differ from a plain program's by a relative error of at most 0.0085.
Values may be sent and summed in bfloat16 or wider, within the bound.
A program may use at most 128 MiB of HBM per device.

v0:
```python
import jax
import jax.numpy as jnp
from jax import lax
from jax.sharding import PartitionSpec as P

IMGTOK = 16


def shifted_2(block, axis, distance):
    devices = range(lax.axis_size(axis))
    route = [(i - distance, i) for i in devices if i - distance in devices]
    return lax.ppermute(block, axis, route)


def routing_tables(place_row, shard_index, image_dev, capacity, ctx_dev, rank_count):
    dest_shard = place_row // ctx_dev
    by_source = dest_shard.reshape(rank_count, image_dev)
    onehot = (
        by_source[:, :, None] == jnp.arange(rank_count, dtype=jnp.int32)[None, None, :]
    ).astype(jnp.int32)
    running = jnp.cumsum(onehot, axis=1) - 1
    slot_index = jnp.sum(running * onehot, axis=2).reshape(-1)
    source_rank = jnp.arange(rank_count * image_dev, dtype=jnp.int32) // image_dev
    send_flat = dest_shard * capacity + slot_index
    recv_flat = source_rank * capacity + slot_index
    is_mine = dest_shard == shard_index
    local_pos = place_row % ctx_dev
    image_marks = (
        jnp.zeros((ctx_dev,), jnp.int32)
        .at[jnp.where(is_mine, local_pos, ctx_dev)]
        .set(1, mode="drop")
    )
    compact_of_pos = jnp.cumsum(image_marks) - 1
    compact = jnp.where(is_mine, compact_of_pos[local_pos], image_dev)
    recv_of_compact = jnp.zeros((image_dev,), jnp.int32).at[compact].set(recv_flat, mode="drop")
    image_pos = jnp.nonzero(image_marks, size=image_dev)[0].astype(jnp.int32)
    own_slots = lax.dynamic_slice_in_dim(send_flat, shard_index * image_dev, image_dev)
    return (own_slots, recv_of_compact, image_pos)


def per_device(image_states, place_index, doc_ids, queries, text_kv, kv_weight, d_out):
    rank_count = lax.axis_size("ctx")
    shard_index = lax.axis_index("ctx")
    ctx_dev = queries.shape[1]
    image_dev = image_states.shape[1]
    head_size = kv_weight.shape[2] // 2
    group_size = queries.shape[2] // head_size
    capacity = IMGTOK * ((image_dev // IMGTOK + rank_count - 1) // rank_count)
    own_slots, recv_of_compact, image_pos = routing_tables(
        place_index[0], shard_index, image_dev, capacity, ctx_dev, rank_count
    )
    weights = kv_weight[0]
    own_states = image_states[0]
    holder = (
        jnp.zeros((rank_count * capacity, own_states.shape[1]), own_states.dtype)
        .at[own_slots]
        .set(own_states)
    )
    arrived = lax.all_to_all(
        holder.reshape(rank_count, capacity, own_states.shape[1]),
        "ctx",
        split_axis=0,
        concat_axis=0,
        tiled=True,
    )
    state_rows = lax.all_gather(
        arrived.reshape(rank_count * capacity, arrived.shape[2])[recv_of_compact],
        "mp",
        axis=1,
        tiled=True,
    )
    image_kv = jnp.dot(state_rows, weights, preferred_element_type=jnp.float32).astype(jnp.bfloat16)
    kv_local = text_kv[0].at[image_pos].set(image_kv)
    earlier = shifted_2(kv_local, "ctx", 1)
    key_window = jnp.concatenate([earlier, kv_local], axis=0)
    key_part = key_window[:, :head_size]
    value_part = key_window[:, head_size:]
    all_docs = doc_ids[0]
    own_docs = lax.dynamic_slice_in_dim(all_docs, shard_index * ctx_dev, ctx_dev)
    prior_docs = lax.dynamic_slice_in_dim(
        all_docs, jnp.maximum(shard_index - 1, 0) * ctx_dev, ctx_dev
    )
    prior_docs = jnp.where(shard_index > 0, prior_docs, -1)
    key_docs = jnp.concatenate([prior_docs, own_docs], axis=0)
    query_pos = jnp.arange(ctx_dev, dtype=jnp.int32)
    key_pos = jnp.arange(2 * ctx_dev, dtype=jnp.int32) - ctx_dev
    allowed = (key_pos[None, :] <= query_pos[:, None]) & (key_docs[None, :] == own_docs[:, None])
    score_scale = head_size ** (-0.5)
    query_heads = queries[0].reshape(ctx_dev, group_size, head_size).transpose(1, 0, 2)
    grad_heads = d_out[0].reshape(ctx_dev, group_size, head_size).transpose(1, 0, 2)

    def one_head(running_sums, head_inputs):
        query_head, grad_head = head_inputs
        scores = (
            lax.dot_general(
                query_head, key_part, (((1,), (1,)), ((), ())), preferred_element_type=jnp.float32
            )
            * score_scale
        )
        scores = jnp.where(allowed, scores, -1e30)
        shifted = jnp.exp(scores - jnp.max(scores, axis=1, keepdims=True))
        shifted = jnp.where(allowed, shifted, 0.0)
        attention = shifted / jnp.sum(shifted, axis=1, keepdims=True)
        attention_low = attention.astype(jnp.bfloat16)
        context = jnp.dot(attention_low, value_part, preferred_element_type=jnp.float32)
        grad_attention = lax.dot_general(
            grad_head, value_part, (((1,), (1,)), ((), ())), preferred_element_type=jnp.float32
        )
        row_delta = jnp.sum(grad_head.astype(jnp.float32) * context, axis=1, keepdims=True)
        grad_scores = (attention * (grad_attention - row_delta)).astype(jnp.bfloat16)
        key_grad = running_sums[0] + score_scale * lax.dot_general(
            grad_scores, query_head, (((0,), (0,)), ((), ())), preferred_element_type=jnp.float32
        )
        value_grad = running_sums[1] + lax.dot_general(
            attention_low, grad_head, (((0,), (0,)), ((), ())), preferred_element_type=jnp.float32
        )
        return ((key_grad, value_grad), context.astype(jnp.bfloat16))

    zero_grads = jnp.zeros((2 * ctx_dev, head_size), jnp.float32)
    (key_grad, value_grad), outputs = lax.scan(
        one_head, (zero_grads, zero_grads), (query_heads, grad_heads)
    )
    attn_out = outputs.transpose(1, 0, 2).reshape(ctx_dev, group_size * head_size)
    kv_grad = jnp.concatenate([key_grad, value_grad], axis=1)
    later = shifted_2(kv_grad[:ctx_dev], "ctx", -1)
    total_grad = kv_grad[ctx_dev:] + later
    grad_low = total_grad[image_pos].astype(jnp.bfloat16)
    partial_value = lax.dot_general(
        grad_low, weights, (((1,), (1,)), ((), ())), preferred_element_type=jnp.float32
    )
    grad_rows = lax.psum_scatter(partial_value, "mp", scatter_dimension=1, tiled=True).astype(
        jnp.bfloat16
    )
    holder = (
        jnp.zeros((rank_count * capacity, grad_rows.shape[1]), grad_rows.dtype)
        .at[recv_of_compact]
        .set(grad_rows)
    )
    back = lax.all_to_all(
        holder.reshape(rank_count, capacity, grad_rows.shape[1]),
        "ctx",
        split_axis=0,
        concat_axis=0,
        tiled=True,
    )
    image_grad = back.reshape(rank_count * capacity, back.shape[2])[own_slots]
    weight_share = lax.psum_scatter(
        lax.dot_general(
            state_rows, grad_low, (((0,), (0,)), ((), ())), preferred_element_type=jnp.float32
        ),
        "ctx",
        scatter_dimension=0,
        tiled=True,
    )
    weight_grad = lax.psum(weight_share, "dp")
    return (attn_out[None], image_grad[None], weight_grad[None])


def solution(mesh):
    in_specs = (
        P("dp", "ctx", "mp"),
        P("dp", None),
        P("dp", None),
        P("dp", "ctx", "mp"),
        P("dp", "ctx", "mp"),
        P("mp", None, None),
        P("dp", "ctx", "mp"),
    )
    out_specs = (P("dp", "ctx", "mp"), P("dp", "ctx", "mp"), P("mp", "ctx", None))
    return jax.shard_map(
        per_device, mesh=mesh, in_specs=in_specs, out_specs=out_specs, check_vma=False
    )
```

profile of v0, /device:TPU:1, one launch (start us, length us, event | category | flops | bytes accessed | tf_op | source)
XLA Modules:
  0.0 721.5 jit_solution(6062487333594903652)
XLA Ops:
  9.8 18.4 %reduce-window.39 = s32[32,32,2,128]{3,1,2,0:T(8,128)S(1)} reduce-window(s32[32,32,2,128]{3,1,2,0:T(8,128)S(1)} %fusion.43, s32[]{:T(128)} %constant.112.clone.1), window={size=1x1x1x128 pad=0_0x0_0x0_0x127_0}, to_apply=%region_7.8 | reduce-window | flops 33292288 | bytes 2097156 | tf_op jit(solution)/shard_map/reduce-window.4
  31.0 3.7 scatter_custom_fusion.2
  34.8 11.9 %all-to-all-start = ((bf16[32,16,2048]{2,1,0:T(8,128)(2,1)}), bf16[32,16,2048]{2,1,0:T(8,128)(2,1)S(1)}, u32[]{:S(2)}, u32[]{:S(2)}) async-start(bf16[32,16,2048]{2,1,0:T(8,128)(2,1)} %bitcast.124), calls=%async_computation | async-start | bytes 4194304 | tf_op jit(solution)/shard_map/all_to_all | solution.py:59
  47.1 30.4 %scatter_custom_fusion = s32[512]{0:T(512)S(1)} fusion(s32[8192]{0:T(1024)S(1)} %bitcast.141, s32[8192]{0:T(1024)S(1)} %broadcast.432, s32[]{:T(128)} %constant.112.clone.1), kind=kCustom, calls=%fused_computation.133 | custom fusion | bytes 2052 | tf_op jit(solution)/shard_map/scatter | solution.py:31
  78.1 51.2 %gather_fusion = s32[8192]{0:T(1024)S(1)} fusion(s32[512]{0:T(512)S(1)} %add_bitcast_fusion.1, s32[8192]{0:T(1024)S(1)} %broadcast_clamp_fusion), kind=kCustom, calls=%fused_computation | custom fusion | bytes 98304 | tf_op jit(solution)/shard_map/gather | solution.py:34
  129.5 30.4 %scatter_custom_fusion.3 = s32[256]{0:T(256)S(1)} fusion(s32[8192]{0:T(1024)S(1)} %bitcast.140, s32[8192]{0:T(1024)S(1)} %fusion.49, s32[]{:T(128)} %constant.112.clone.1), kind=kCustom, calls=%fused_computation.136 | custom fusion | bytes 1028 | tf_op jit(solution)/shard_map/scatter | solution.py:35
  163.6 4.1 scatter_custom_fusion.1
  169.0 45.8 %all-gather.3.cloned.1.call-done = bf16[256,8192]{1,0:T(8,128)(2,1)} async-done(((bf16[256,2048]{1,0:T(8,128)(2,1)}), bf16[256,8192]{1,0:T(8,128)(2,1)}) %all-gather.3.cloned.1.call-update) | async-done | bytes 4194320 | tf_op jit(solution)/shard_map/all_gather | solution.py:66
  214.8 4.7 fusion.32
  221.3 3.8 collective-permute-start
  231.0 86.4 %while.15 = (s32[]{:T(128)}, f32[1024,128]{1,0:T(8,128)}, f32[1024,128]{1,0:T(8,128)}, bf16[8,512,128]{1,2,0:T(8,128)(2,1)}, bf16[8,512,128]{1,2,0:T(8,128)(2,1)...) while((s32[]{:T(128)}, f32[1024,128]{1,0:T(8,128)}, ...), condition=%wide.region_19.20_spmd.clone, body=%wide.region_15.19_spmd.clone.sunk | while | flops 686160384 | bytes 18659980 | solution.py:120
  268.8 2.8 fusion.96
  279.7 2.8 fusion.96
  290.5 2.8 fusion.96
  301.4 2.8 fusion.96
  312.2 2.8 fusion.96
  320.9 13.5 %collective-permute-done.1 = f32[512,256]{1,0:T(8,128)S(1)} collective-permute-done((f32[512,256]{1,0:T(8,128)S(1)}, f32[512,256]{1,0:T(8,128)S(1)}, u32[]{:S(2)}, u32[]{:S(2)}) %collective-permute-start.1) | collective-permute-done | bytes 524320 | tf_op jit(solution)/shard_map/ppermute | solution.py:12
  335.6 6.7 fusion.28
  342.4 6.7 fusion.67
  349.2 80.5 %reduce-scatter.3.cloned.1.call-done = f32[256,2048]{1,0:T(8,128)} async-done(((f32[256,8192]{1,0:T(8,128)}), f32[256,2048]{1,0:T(8,128)}) %reduce-scatter.3.cloned.1.call-update) | async-done | bytes 2097168 | tf_op jit(solution)/shard_map/reduce_scatter | solution.py:131
  429.6 4.8 scatter_custom_fusion.5
  434.4 9.5 %all-to-all-start.1 = ((bf16[32,16,2048]{2,1,0:T(8,128)(2,1)}), bf16[32,16,2048]{2,1,0:T(8,128)(2,1)S(1)}, u32[]{:S(2)}, u32[]{:S(2)}) async-start(bf16[32,16,2048]{2,1,0:T(8,128)(2,1)} %bitcast.125), calls=%async_computation.2 | async-start | bytes 4194304 | tf_op jit(solution)/shard_map/all_to_all | solution.py:139
  444.0 234.5 %reduce-scatter.5.cloned.1.call-done = f32[256,256]{1,0:T(8,128)} async-done(((f32[8192,256]{1,0:T(8,128)}), f32[256,256]{1,0:T(8,128)}) %reduce-scatter.5.cloned.1.call-update) | async-done | bytes 262160 | tf_op jit(solution)/shard_map/reduce_scatter | solution.py:147
  683.2 30.1 %all-reduce.2.cloned.1.call-done = f32[1,256,256]{2,1,0:T(8,128)} async-done(((f32[1,256,256]{2,1,0:T(8,128)}), f32[1,256,256]{2,1,0:T(8,128)}) %all-reduce.2.cloned.1.call-update) | async-done | bytes 262160 | tf_op jit(solution)/shard_map/psum | solution.py:155
  (139 shorter events, 102.6 us)
Async XLA Ops:
  7.2 23.9 %copy-start = (bf16[1,256,2048]{2,1,0:T(8,128)(2,1)S(1)}, bf16[1,256,2048]{2,1,0:T(8,128)(2,1)}, u32[]{:S(2)}) copy-start(bf16[1,256,2048]{2,1,0:T(8,128)(2,1)} %param.9) | copy-start | bytes 3145732
  28.2 1.4 copy-start.2
  34.8 125.1 %all-to-all-start = ((bf16[32,16,2048]{2,1,0:T(8,128)(2,1)}), bf16[32,16,2048]{2,1,0:T(8,128)(2,1)S(1)}, u32[]{:S(2)}, u32[]{:S(2)}) async-start(bf16[32,16,2048]{2,1,0:T(8,128)(2,1)} %bitcast.124), calls=%async_computation | async-start | bytes 4194304 | tf_op jit(solution)/shard_map/all_to_all | solution.py:59
  46.6 168.1 %all-gather.3.cloned.1.call-start = ((), (), s32[]{:S(2)}) async-start(), calls=%async_computation.7 | async-start | bytes 5242880 | tf_op jit(solution)/shard_map/all_gather | solution.py:66
  162.3 267.3 %reduce-scatter.3.cloned.1.call-start = ((), (), s32[]{:S(2)}) async-start(), calls=%async_computation.4 | async-start | bytes 10485760 | tf_op jit(solution)/shard_map/reduce_scatter | solution.py:131
  169.0 50.5 %copy-start.1 = (bf16[1,512,256]{2,1,0:T(8,128)(2,1)S(1)}, bf16[1,512,256]{2,1,0:T(8,128)(2,1)}, u32[]{:S(2)}) copy-start(bf16[1,512,256]{2,1,0:T(8,128)(2,1)} %param.13) | copy-start | bytes 786436
  219.5 5.7 copy-start.3
  219.5 7.0 copy-start.4
  221.3 7.9 %collective-permute-start = (bf16[512,256]{1,0:T(8,128)(2,1)S(1)}, bf16[512,256]{1,0:T(8,128)(2,1)}, u32[]{:S(2)}, u32[]{:S(2)}) collective-permute-start(bf16[512,256]{1,0:T(8,128)(2,1)S(1)} %scatter_fusion), channel_id=1, source_target_pairs={{0,4},{4,8},{8,12},{12,16},{16,20},{20,24},{24,28},{28,32},{32,36}... | collective-permute-start | bytes 786440 | tf_op jit(solution)/shard_map/ppermute | solution.py:12
  319.6 14.8 %collective-permute-start.1 = (f32[512,256]{1,0:T(8,128)S(1)}, f32[512,256]{1,0:T(8,128)S(1)}, u32[]{:S(2)}, u32[]{:S(2)}) collective-permute-start(f32[512,256]{1,0:T(8,128)S(1)} %slice.64), channel_id=1, source_target_pairs={{4,0},{8,4},{12,8},{16,12},{20,16},{24,20},{28,24},{32,28},{36,32}... | collective-permute-start | bytes 1572872 | tf_op jit(solution)/shard_map/ppermute | solution.py:12
  342.4 336.2 %reduce-scatter.5.cloned.1.call-start = ((), (), s32[]{:S(2)}) async-start(), calls=%async_computation.5 | async-start | bytes 8650752 | tf_op jit(solution)/shard_map/reduce_scatter | solution.py:147
  434.4 246.4 %all-to-all-start.1 = ((bf16[32,16,2048]{2,1,0:T(8,128)(2,1)}), bf16[32,16,2048]{2,1,0:T(8,128)(2,1)S(1)}, u32[]{:S(2)}, u32[]{:S(2)}) async-start(bf16[32,16,2048]{2,1,0:T(8,128)(2,1)} %bitcast.125), calls=%async_computation.2 | async-start | bytes 4194304 | tf_op jit(solution)/shard_map/all_to_all | solution.py:139
  444.0 269.3 %all-reduce.2.cloned.1.call-start = ((), (), s32[]{:S(2)}) async-start(), calls=%async_computation.6 | async-start | bytes 524288 | tf_op jit(solution)/shard_map/psum | solution.py:155
Sparse Core Ops, SparseCore 0:
  162.4 52.3 all-gather.2
  342.5 87.0 reduce-scatter.2
  433.6 244.8 reduce-scatter.4
  681.0 32.2 all-reduce.1
where the time goes:
time: 723 us; the launch traced here: 721 us
  waiting for transfers between devices  405 us (56%)
  local copies, waits for them, and re-layouts  141 us (20%)
  matrix products  84.7 us (12%)
  other arithmetic  49.5 us (7%)
  starting transfers between devices  26.7 us (4%)
  between operations  14.1 us (2%)
    reduce_scatter x1, waiting for transfers between devices, per_device(): lax.psum_scatter(lax.dot_general(state_rows, grad_low, (((0,), (0,)), (()...  235 us
    reduce_scatter x1, waiting for transfers between devices, per_device(): lax.psum_scatter(partial_value, 'mp', scatter_dimension=1, tiled=True)  80.5 us
    gather x1, local copies, waits for them, and re-layouts, routing_tables(): compact = jnp.where(is_mine, compact_of_pos[local_pos], image_dev)  51.2 us
    all_gather x1, waiting for transfers between devices, per_device(): lax.all_gather(arrived.reshape(rank_count * capacity, arrived.shape[2])[r...  45.8 us
    scatter x1, local copies, waits for them, and re-layouts, routing_tables(): jnp.zeros((image_dev,), jnp.int32).at[compact].set(recv_flat, mode='drop')  30.4 us
    scatter x1, local copies, waits for them, and re-layouts, routing_tables(): image_marks = jnp.zeros((ctx_dev,), jnp.int32).at[jnp.where(is_mine, loca...  30.4 us
    psum x1, waiting for transfers between devices, per_device(): weight_grad = lax.psum(weight_share, 'dp')  30.1 us
    dot_general x8, matrix products, one_head(): lax.dot_general(grad_scores, query_head, (((0,), (0,)), ((), ())), prefer...  21.9 us
  transfers between devices with their start and end apart: 8, of which 6 were waited for; matrix products, arithmetic and copies ran while one was open for 19% of the time, Pallas kernels for 0%

commit v1 on v0

--- a/solution.py
+++ b/solution.py
@@ -152,7 +152,8 @@
         scatter_dimension=0,
         tiled=True,
     )
-    weight_grad = lax.psum(weight_share, "dp")
+    parts = lax.all_gather(weight_share, "dp")
+    weight_grad = jnp.sum(parts, axis=0)
     return (attn_out[None], image_grad[None], weight_grad[None])
 
 

time: 723 us -> 699 us (0.967)
  waiting for transfers between devices: 405 us -> 373 us
  blocking collectives: 0 us -> 8.4 us
    psum x1 -> x0, waiting for transfers between devices: 30.1 us -> none  [per_device(): weight_grad = lax.psum(weight_share, 'dp')]
    all_gather x0 -> x1, blocking collectives: none -> 8.4 us  [per_device(): parts = lax.all_gather(weight_share, 'dp')]
  transfers between devices with their start and end apart: 8 -> 7, of which waited for: 6 -> 5; matrix products, arithmetic and copies ran while one was open for 19% -> 20% of each run, Pallas kernels for 0% -> 0%
where the time goes in v1:
time: 699 us; the launch traced here: 698 us
  waiting for transfers between devices  373 us (53%)
  local copies, waits for them, and re-layouts  140 us (20%)
  matrix products  84.7 us (12%)
  other arithmetic  51.3 us (7%)
  starting transfers between devices  26.6 us (4%)
  between operations  14.1 us (2%)
  blocking collectives  8.4 us (1%)
    reduce_scatter x1, waiting for transfers between devices, per_device(): lax.psum_scatter(lax.dot_general(state_rows, grad_low, (((0,), (0,)), (()...  232 us
    reduce_scatter x1, waiting for transfers between devices, per_device(): lax.psum_scatter(partial_value, 'mp', scatter_dimension=1, tiled=True)  80.5 us
    gather x1, local copies, waits for them, and re-layouts, routing_tables(): compact = jnp.where(is_mine, compact_of_pos[local_pos], image_dev)  51.2 us
    all_gather x1, waiting for transfers between devices, per_device(): lax.all_gather(arrived.reshape(rank_count * capacity, arrived.shape[2])[r...  45.8 us
    scatter x1, local copies, waits for them, and re-layouts, routing_tables(): jnp.zeros((image_dev,), jnp.int32).at[compact].set(recv_flat, mode='drop')  30.4 us
    scatter x1, local copies, waits for them, and re-layouts, routing_tables(): image_marks = jnp.zeros((ctx_dev,), jnp.int32).at[jnp.where(is_mine, loca...  30.4 us
    dot_general x8, matrix products, one_head(): lax.dot_general(grad_scores, query_head, (((0,), (0,)), ((), ())), prefer...  21.9 us
    another operation x10, other arithmetic  19.7 us
  transfers between devices with their start and end apart: 7, of which 5 were waited for; matrix products, arithmetic and copies ran while one was open for 20% of the time, Pallas kernels for 0%

profile of v1, /device:TPU:1, one launch (start us, length us, event | category | flops | bytes accessed | tf_op | source)
XLA Modules:
  0.0 697.6 jit_solution(15067543911213623185)
XLA Ops:
  9.8 18.4 %reduce-window.39 = s32[32,32,2,128]{3,1,2,0:T(8,128)S(1)} reduce-window(s32[32,32,2,128]{3,1,2,0:T(8,128)S(1)} %fusion.43, s32[]{:T(128)} %constant.113.clone.1), window={size=1x1x1x128 pad=0_0x0_0x0_0x127_0}, to_apply=%region_7.8 | reduce-window | flops 33292288 | bytes 2097156 | tf_op jit(solution)/shard_map/reduce-window.4
  31.0 3.7 scatter_custom_fusion.2
  34.8 11.9 %all-to-all-start = ((bf16[32,16,2048]{2,1,0:T(8,128)(2,1)}), bf16[32,16,2048]{2,1,0:T(8,128)(2,1)S(1)}, u32[]{:S(2)}, u32[]{:S(2)}) async-start(bf16[32,16,2048]{2,1,0:T(8,128)(2,1)} %bitcast.125), calls=%async_computation | async-start | bytes 4194304 | tf_op jit(solution)/shard_map/all_to_all | solution.py:59
  47.1 30.4 %scatter_custom_fusion = s32[512]{0:T(512)S(1)} fusion(s32[8192]{0:T(1024)S(1)} %bitcast.143, s32[8192]{0:T(1024)S(1)} %broadcast.432, s32[]{:T(128)} %constant.113.clone.1), kind=kCustom, calls=%fused_computation.133 | custom fusion | bytes 2052 | tf_op jit(solution)/shard_map/scatter | solution.py:31
  78.1 51.2 %gather_fusion = s32[8192]{0:T(1024)S(1)} fusion(s32[512]{0:T(512)S(1)} %add_bitcast_fusion.1, s32[8192]{0:T(1024)S(1)} %broadcast_clamp_fusion), kind=kCustom, calls=%fused_computation | custom fusion | bytes 98304 | tf_op jit(solution)/shard_map/gather | solution.py:34
  129.5 30.4 %scatter_custom_fusion.3 = s32[256]{0:T(256)S(1)} fusion(s32[8192]{0:T(1024)S(1)} %bitcast.142, s32[8192]{0:T(1024)S(1)} %fusion.49, s32[]{:T(128)} %constant.113.clone.1), kind=kCustom, calls=%fused_computation.136 | custom fusion | bytes 1028 | tf_op jit(solution)/shard_map/scatter | solution.py:35
  163.6 4.1 scatter_custom_fusion.1
  169.0 45.8 %all-gather.4.cloned.1.call-done = bf16[256,8192]{1,0:T(8,128)(2,1)} async-done(((bf16[256,2048]{1,0:T(8,128)(2,1)}), bf16[256,8192]{1,0:T(8,128)(2,1)}) %all-gather.4.cloned.1.call-update) | async-done | bytes 4194320 | tf_op jit(solution)/shard_map/all_gather | solution.py:66
  214.8 4.7 fusion.32
  221.3 3.8 collective-permute-start
  231.0 86.4 %while.15 = (s32[]{:T(128)}, f32[1024,128]{1,0:T(8,128)}, f32[1024,128]{1,0:T(8,128)}, bf16[8,512,128]{1,2,0:T(8,128)(2,1)}, bf16[8,512,128]{1,2,0:T(8,128)(2,1)...) while((s32[]{:T(128)}, f32[1024,128]{1,0:T(8,128)}, ...), condition=%wide.region_19.20_spmd.clone, body=%wide.region_15.19_spmd.clone.sunk | while | flops 686160384 | bytes 18659980 | solution.py:120
  268.8 2.8 fusion.96
  279.7 2.8 fusion.96
  290.5 2.8 fusion.96
  301.4 2.8 fusion.96
  312.2 2.8 fusion.96
  320.9 13.5 %collective-permute-done.1 = f32[512,256]{1,0:T(8,128)S(1)} collective-permute-done((f32[512,256]{1,0:T(8,128)S(1)}, f32[512,256]{1,0:T(8,128)S(1)}, u32[]{:S(2)}, u32[]{:S(2)}) %collective-permute-start.1) | collective-permute-done | bytes 524320 | tf_op jit(solution)/shard_map/ppermute | solution.py:12
  335.6 6.7 fusion.28
  342.4 6.7 fusion.67
  349.2 80.5 %reduce-scatter.3.cloned.1.call-done = f32[256,2048]{1,0:T(8,128)} async-done(((f32[256,8192]{1,0:T(8,128)}), f32[256,2048]{1,0:T(8,128)}) %reduce-scatter.3.cloned.1.call-update) | async-done | bytes 2097168 | tf_op jit(solution)/shard_map/reduce_scatter | solution.py:131
  429.6 4.8 scatter_custom_fusion.5
  434.4 9.5 %all-to-all-start.1 = ((bf16[32,16,2048]{2,1,0:T(8,128)(2,1)}), bf16[32,16,2048]{2,1,0:T(8,128)(2,1)S(1)}, u32[]{:S(2)}, u32[]{:S(2)}) async-start(bf16[32,16,2048]{2,1,0:T(8,128)(2,1)} %bitcast.126), calls=%async_computation.2 | async-start | bytes 4194304 | tf_op jit(solution)/shard_map/all_to_all | solution.py:139
  446.3 232.3 %reduce-scatter.5.cloned.1.call-done = f32[256,256]{1,0:T(8,128)} async-done(((f32[8192,256]{1,0:T(8,128)}), f32[256,256]{1,0:T(8,128)}) %reduce-scatter.5.cloned.1.call-update) | async-done | bytes 262160 | tf_op jit(solution)/shard_map/reduce_scatter | solution.py:147
  678.5 8.4 %all-gather.1 = f32[512,256]{1,0:T(8,128)} all-gather(f32[256,256]{1,0:T(8,128)} %reduce-scatter.5.cloned.1.call-done), channel_id=3, replica_groups=mesh['dp'=2,'ctx'=32,'mp'=4] {'dp'}, dimensions={0}, use_global_device_ids=true | all-gather | bytes 786432 | tf_op jit(solution)/shard_map/all_gather | solution.py:155
  (137 shorter events, 102.6 us)
Async XLA Ops:
  7.2 23.9 %copy-start = (bf16[1,256,2048]{2,1,0:T(8,128)(2,1)S(1)}, bf16[1,256,2048]{2,1,0:T(8,128)(2,1)}, u32[]{:S(2)}) copy-start(bf16[1,256,2048]{2,1,0:T(8,128)(2,1)} %param.9) | copy-start | bytes 3145732
  28.2 1.4 copy-start.2
  34.8 125.1 %all-to-all-start = ((bf16[32,16,2048]{2,1,0:T(8,128)(2,1)}), bf16[32,16,2048]{2,1,0:T(8,128)(2,1)S(1)}, u32[]{:S(2)}, u32[]{:S(2)}) async-start(bf16[32,16,2048]{2,1,0:T(8,128)(2,1)} %bitcast.125), calls=%async_computation | async-start | bytes 4194304 | tf_op jit(solution)/shard_map/all_to_all | solution.py:59
  46.6 168.1 %all-gather.4.cloned.1.call-start = ((), (), s32[]{:S(2)}) async-start(), calls=%async_computation.6 | async-start | bytes 5242880 | tf_op jit(solution)/shard_map/all_gather | solution.py:66
  162.3 267.3 %reduce-scatter.3.cloned.1.call-start = ((), (), s32[]{:S(2)}) async-start(), calls=%async_computation.4 | async-start | bytes 10485760 | tf_op jit(solution)/shard_map/reduce_scatter | solution.py:131
  169.0 50.5 %copy-start.1 = (bf16[1,512,256]{2,1,0:T(8,128)(2,1)S(1)}, bf16[1,512,256]{2,1,0:T(8,128)(2,1)}, u32[]{:S(2)}) copy-start(bf16[1,512,256]{2,1,0:T(8,128)(2,1)} %param.13) | copy-start | bytes 786436
  219.5 5.7 copy-start.3
  219.5 7.0 copy-start.4
  221.3 7.9 %collective-permute-start = (bf16[512,256]{1,0:T(8,128)(2,1)S(1)}, bf16[512,256]{1,0:T(8,128)(2,1)}, u32[]{:S(2)}, u32[]{:S(2)}) collective-permute-start(bf16[512,256]{1,0:T(8,128)(2,1)S(1)} %scatter_fusion), channel_id=1, source_target_pairs={{0,4},{4,8},{8,12},{12,16},{16,20},{20,24},{24,28},{28,32},{32,36}... | collective-permute-start | bytes 786440 | tf_op jit(solution)/shard_map/ppermute | solution.py:12
  319.6 14.8 %collective-permute-start.1 = (f32[512,256]{1,0:T(8,128)S(1)}, f32[512,256]{1,0:T(8,128)S(1)}, u32[]{:S(2)}, u32[]{:S(2)}) collective-permute-start(f32[512,256]{1,0:T(8,128)S(1)} %slice.64), channel_id=1, source_target_pairs={{4,0},{8,4},{12,8},{16,12},{20,16},{24,20},{28,24},{32,28},{36,32}... | collective-permute-start | bytes 1572872 | tf_op jit(solution)/shard_map/ppermute | solution.py:12
  342.4 336.2 %reduce-scatter.5.cloned.1.call-start = ((), (), s32[]{:S(2)}) async-start(), calls=%async_computation.5 | async-start | bytes 8650752 | tf_op jit(solution)/shard_map/reduce_scatter | solution.py:147
  434.4 254.3 %all-to-all-start.1 = ((bf16[32,16,2048]{2,1,0:T(8,128)(2,1)}), bf16[32,16,2048]{2,1,0:T(8,128)(2,1)S(1)}, u32[]{:S(2)}, u32[]{:S(2)}) async-start(bf16[32,16,2048]{2,1,0:T(8,128)(2,1)} %bitcast.126), calls=%async_computation.2 | async-start | bytes 4194304 | tf_op jit(solution)/shard_map/all_to_all | solution.py:139
Sparse Core Ops, SparseCore 0:
  162.4 52.3 all-gather.3
  342.5 87.0 reduce-scatter.2
  433.6 244.8 reduce-scatter.4
